TPU v7x, 32 devices: a whole 2x2x4 slice. The times are simulated.
32 devices in a mesh: rows: 8 (over z, y), heads: 4 (over x, core).
Axes of the slice: x: 2, y: 2, z: 4, core: 2. Of those that a mesh axis runs over, the one named last changes fastest.
Arguments:
- frames: bfloat16 [24, 800, 640], P('rows'), may hold values from -6 to 6
- segment_ids: int32 [24, 800], P('rows'), may hold values from -1 to 3, as said below
- cotangent: bfloat16 [24, 800, 640], P('rows'), may hold values from -6 to 6
- query_weight: bfloat16 [640, 768], P(None, 'heads'), may hold values from -0.25 to 0.25
- query_bias: float32 [768], P('heads'), may hold values from -3 to 3
- key_weight: bfloat16 [640, 768], P(None, 'heads'), may hold values from -0.25 to 0.25
- value_weight: bfloat16 [640, 768], P(None, 'heads'), may hold values from -0.25 to 0.25
- value_bias: float32 [768], P('heads'), may hold values from -3 to 3
- output_weight: bfloat16 [768, 640], P('heads'), may hold values from -2 to 2
- output_bias: float32 [640], replicated, may hold values from -3 to 3
- first_gain: float32 [640], replicated, may hold values from 0.1 to 1.9
- first_shift: float32 [640], replicated, may hold values from -3 to 3
- inner_weight: bfloat16 [640, 3072], P(None, 'heads'), may hold values from -0.25 to 0.25
- inner_bias: float32 [3072], P('heads'), may hold values from -3 to 3
- outer_weight: bfloat16 [3072, 640], P('heads'), may hold values from -0.1875 to 0.1875
- outer_bias: float32 [640], replicated, may hold values from -3 to 3
- second_gain: float32 [640], replicated, may hold values from 0.1 to 1.9
- second_shift: float32 [640], replicated, may hold values from -3 to 3
Outputs:
- layer_out: bfloat16 [24, 800, 640], P('rows')
- frames_grad: bfloat16 [24, 800, 640], P('rows')
- query_grad: float32 [640, 768], P(None, 'heads')
- querybias_grad: float32 [768], P('heads')
- key_grad: float32 [640, 768], P(None, 'heads')
- value_grad: float32 [640, 768], P(None, 'heads')
- valuebias_grad: float32 [768], P('heads')
- output_grad: float32 [768, 640], P('heads')
- outputbias_grad: float32 [640], replicated
- firstgain_grad: float32 [640], replicated
- firstshift_grad: float32 [640], replicated
- inner_grad: float32 [640, 3072], P(None, 'heads')
- innerbias_grad: float32 [3072], P('heads')
- outer_grad: float32 [3072, 640], P('heads')
- outerbias_grad: float32 [640], replicated
- secondgain_grad: float32 [640], replicated
- secondshift_grad: float32 [640], replicated
Inputs may be any that keep to these rules, and one draw needn't show every extreme that they name: `segment_ids`: along each row the ids run 0, 1, 2, 3 in order, each segment nonempty, and the row ends with 1 to 200 pad frames of id -1.
All inputs are finite; a program needn't handle non-finite values.
Results may differ from a plain program's by a relative error of at most 0.024.
Values may be sent and summed in bfloat16 or wider, within the bound.
No kernel may reach another device: no remote copies, remote signals or barrier semaphores. Data moves between devices by JAX's collectives and lax.ppermute only.
A program may use at most 192 MiB of HBM per device.

v0:
```python
import jax
import jax.numpy as jnp
from jax import lax
from jax.sharding import PartitionSpec as P

HEADS_LIVE = 10
HEAD_DIM = 64
FF_LIVE = 2240


norm_eps = 1e-05


def exact_gelu(value):
    return jax.nn.gelu(value, approximate=False)


def layer_stats(value):
    centre = value - jnp.mean(value, axis=-1, keepdims=True)
    inverse = lax.rsqrt(jnp.mean(centre * centre, axis=-1, keepdims=True) + norm_eps)
    return (centre * inverse, inverse)


def norm_back(grad_out, normal, inverse, gain):
    scaled = grad_out * gain
    return inverse * (
        scaled
        - jnp.mean(scaled, axis=-1, keepdims=True)
        - normal * jnp.mean(scaled * normal, axis=-1, keepdims=True)
    )


def masked_scores(queries, keys_low, row_ids):
    scores = jnp.einsum(
        "qhd,khd->hqk", queries, keys_low, preferred_element_type=jnp.float32
    ) * HEAD_DIM ** (-0.5)
    allowed = (row_ids[:, None] == row_ids[None, :])[None]
    return jnp.where(allowed, scores, -1e30)


def attend(packed):
    queries, keys_low, values_low, row_ids = packed
    scores = masked_scores(queries, keys_low, row_ids)
    highest = jnp.max(scores, axis=-1, keepdims=True)
    log_total = highest + jnp.log(jnp.sum(jnp.exp(scores - highest), axis=-1, keepdims=True))
    probs = jnp.exp(scores - log_total).astype(jnp.bfloat16)
    context = jnp.einsum("hqk,khd->qhd", probs, values_low, preferred_element_type=jnp.float32)
    return (context.astype(jnp.bfloat16), log_total)


def attend_back(packed):
    queries, keys_low, values_low, row_ids, log_total, grad_context = packed
    probs_full = jnp.exp(masked_scores(queries, keys_low, row_ids) - log_total)
    probs = probs_full.astype(jnp.bfloat16)
    grad_values = jnp.einsum(
        "hqk,qhd->khd", probs, grad_context, preferred_element_type=jnp.float32
    )
    grad_probs = jnp.einsum(
        "qhd,khd->hqk", grad_context, values_low, preferred_element_type=jnp.float32
    )
    centred = grad_probs - jnp.sum(grad_probs * probs_full, axis=-1, keepdims=True)
    grad_scores = (probs_full * centred).astype(jnp.bfloat16)
    score_scale = HEAD_DIM ** (-0.5)
    grad_queries = (
        jnp.einsum("hqk,khd->qhd", grad_scores, keys_low, preferred_element_type=jnp.float32)
        * score_scale
    )
    grad_keys = (
        jnp.einsum("hqk,qhd->khd", grad_scores, queries, preferred_element_type=jnp.float32)
        * score_scale
    )
    return (
        grad_queries.astype(jnp.bfloat16),
        grad_keys.astype(jnp.bfloat16),
        grad_values.astype(jnp.bfloat16),
    )


def per_device(
    frames,
    segment_ids,
    cotangent,
    query_weight,
    query_bias,
    key_weight,
    value_weight,
    value_bias,
    output_weight,
    output_bias,
    first_gain,
    first_shift,
    inner_weight,
    inner_bias,
    outer_weight,
    outer_bias,
    second_gain,
    second_shift,
):
    group_size = lax.axis_size("heads")
    position = lax.axis_index("heads")
    row_count, row_length, model_width = frames.shape
    share_len = row_length // group_size
    heads_here = query_weight.shape[1] // HEAD_DIM
    slot_width = heads_here * HEAD_DIM
    per_head = FF_LIVE // HEADS_LIVE
    hidden_slots = inner_weight.shape[1]
    hidden_cap = min(hidden_slots, (HEADS_LIVE + group_size - 1) // group_size * per_head)
    live_heads = HEADS_LIVE // group_size + (position < HEADS_LIVE % group_size).astype(jnp.int32)
    head_mask = (jnp.arange(slot_width, dtype=jnp.int32) // HEAD_DIM < live_heads).astype(
        jnp.float32
    )[:, None]
    hidden_mask = (jnp.arange(hidden_cap, dtype=jnp.int32) < live_heads * per_head).astype(
        jnp.float32
    )[:, None]
    out_weight = output_weight * head_mask.astype(jnp.bfloat16)
    down_weight = outer_weight[:hidden_cap] * hidden_mask.astype(jnp.bfloat16)
    up_weight = inner_weight[:, :hidden_cap]
    up_bias = inner_bias[:hidden_cap]
    full_shape = (row_count, row_length, model_width)

    def own_part(value):
        return lax.dynamic_slice_in_dim(value, position * share_len, share_len, 1)

    def narrow(value):
        return own_part(value)

    def spread(value):
        return lax.all_gather(value, "heads", axis=1, tiled=True)

    def forward_total(part):
        return lax.psum_scatter(
            part.astype(jnp.bfloat16), "heads", scatter_dimension=1, tiled=True
        ).astype(jnp.float32)

    def backward_total(part):
        return lax.psum_scatter(
            part.astype(jnp.bfloat16), "heads", scatter_dimension=1, tiled=True
        ).astype(jnp.float32)

    flat_frames = frames.reshape(row_count * row_length, model_width)
    queries = (
        jnp.dot(flat_frames, query_weight, preferred_element_type=jnp.float32) + query_bias
    ).astype(jnp.bfloat16)
    keys_low = jnp.dot(flat_frames, key_weight, preferred_element_type=jnp.float32).astype(
        jnp.bfloat16
    )
    values_low = (
        jnp.dot(flat_frames, value_weight, preferred_element_type=jnp.float32) + value_bias
    ).astype(jnp.bfloat16)
    head_shape = (row_count, row_length, heads_here, HEAD_DIM)
    query_rows = queries.reshape(head_shape)
    key_rows = keys_low.reshape(head_shape)
    value_rows = values_low.reshape(head_shape)
    context, log_total = lax.map(attend, (query_rows, key_rows, value_rows, segment_ids))
    context_flat = context.reshape(row_count * row_length, slot_width)
    attn_part = jnp.dot(context_flat, out_weight, preferred_element_type=jnp.float32).reshape(
        full_shape
    )
    hidden_one = narrow(frames).astype(jnp.float32) + forward_total(attn_part) + output_bias
    normal_one, inverse_one = layer_stats(hidden_one)
    normed_one = normal_one * first_gain + first_shift
    normed_low = spread(normed_one.astype(jnp.bfloat16)).reshape(
        row_count * row_length, model_width
    )
    inner_pre = jnp.dot(normed_low, up_weight, preferred_element_type=jnp.float32) + up_bias
    active, gelu_pull = jax.vjp(exact_gelu, inner_pre)
    active_low = active.astype(jnp.bfloat16)
    ffn_part = jnp.dot(active_low, down_weight, preferred_element_type=jnp.float32).reshape(
        full_shape
    )
    hidden_two = normed_one + forward_total(ffn_part) + outer_bias
    normal_two, inverse_two = layer_stats(hidden_two)
    live_rows = narrow((segment_ids >= 0).astype(jnp.float32)[:, :, None])
    final_out = (normal_two * second_gain + second_shift) * live_rows
    layer_out = spread(final_out.astype(jnp.bfloat16))
    grad_final = narrow(cotangent).astype(jnp.float32) * live_rows
    secondgain_part = jnp.sum(grad_final * normal_two, axis=(0, 1))
    secondshift_part = jnp.sum(grad_final, axis=(0, 1))
    grad_hidden_two = norm_back(grad_final, normal_two, inverse_two, second_gain)
    outerbias_part = jnp.sum(grad_hidden_two, axis=(0, 1))
    grad_ffn = spread(grad_hidden_two.astype(jnp.bfloat16)).reshape(
        row_count * row_length, model_width
    )
    outer_part = (
        jnp.einsum("tc,td->cd", active_low, grad_ffn, preferred_element_type=jnp.float32)
        * hidden_mask
    )
    grad_active = jnp.einsum("td,cd->tc", grad_ffn, down_weight, preferred_element_type=jnp.float32)
    grad_inner = gelu_pull(grad_active)[0].astype(jnp.bfloat16)
    inner_part = jnp.einsum("td,tc->dc", normed_low, grad_inner, preferred_element_type=jnp.float32)
    innerbias_part = jnp.sum(grad_inner, axis=0, dtype=jnp.float32)
    grad_back = jnp.einsum(
        "tc,dc->td", grad_inner, up_weight, preferred_element_type=jnp.float32
    ).reshape(full_shape)
    grad_normed = grad_hidden_two + backward_total(grad_back)
    firstgain_part = jnp.sum(grad_normed * normal_one, axis=(0, 1))
    firstshift_part = jnp.sum(grad_normed, axis=(0, 1))
    grad_hidden_one = norm_back(grad_normed, normal_one, inverse_one, first_gain)
    outputbias_part = jnp.sum(grad_hidden_one, axis=(0, 1))
    grad_attn = spread(grad_hidden_one.astype(jnp.bfloat16)).reshape(
        row_count * row_length, model_width
    )
    output_part = (
        jnp.einsum("tk,td->kd", context_flat, grad_attn, preferred_element_type=jnp.float32)
        * head_mask
    )
    grad_context = jnp.einsum(
        "td,kd->tk", grad_attn, out_weight, preferred_element_type=jnp.float32
    ).astype(jnp.bfloat16)
    grad_query_rows, grad_key_rows, grad_value_rows = lax.map(
        attend_back,
        (
            query_rows,
            key_rows,
            value_rows,
            segment_ids,
            log_total,
            grad_context.reshape(head_shape),
        ),
    )
    grad_queries = grad_query_rows.reshape(row_count * row_length, slot_width)
    grad_keys = grad_key_rows.reshape(row_count * row_length, slot_width)
    grad_values = grad_value_rows.reshape(row_count * row_length, slot_width)
    query_part = jnp.einsum(
        "td,tk->dk", flat_frames, grad_queries, preferred_element_type=jnp.float32
    )
    querybias_part = jnp.sum(grad_queries, axis=0, dtype=jnp.float32)
    key_part = jnp.einsum("td,tk->dk", flat_frames, grad_keys, preferred_element_type=jnp.float32)
    value_part = jnp.einsum(
        "td,tk->dk", flat_frames, grad_values, preferred_element_type=jnp.float32
    )
    valuebias_part = jnp.sum(grad_values, axis=0, dtype=jnp.float32)
    input_back = (
        jnp.einsum("tk,dk->td", grad_queries, query_weight, preferred_element_type=jnp.float32)
        + jnp.einsum("tk,dk->td", grad_keys, key_weight, preferred_element_type=jnp.float32)
        + jnp.einsum("tk,dk->td", grad_values, value_weight, preferred_element_type=jnp.float32)
    )
    frames_grad = spread(
        (grad_hidden_one + backward_total(input_back.reshape(full_shape))).astype(jnp.bfloat16)
    )
    norm_sums = lax.psum(
        (
            outputbias_part,
            firstgain_part,
            firstshift_part,
            outerbias_part,
            secondgain_part,
            secondshift_part,
        ),
        ("rows", "heads"),
    )
    (
        query_sum,
        querybias_sum,
        key_sum,
        value_sum,
        valuebias_sum,
        output_sum,
        inner_sum,
        innerbias_sum,
        outer_sum,
    ) = lax.psum(
        (
            query_part,
            querybias_part,
            key_part,
            value_part,
            valuebias_part,
            output_part,
            inner_part,
            innerbias_part,
            outer_part,
        ),
        "rows",
    )
    padding = hidden_slots - hidden_cap
    inner_full = jnp.pad(inner_sum, ((0, 0), (0, padding)))
    innerbias_full = jnp.pad(innerbias_sum, ((0, padding),))
    outer_full = jnp.pad(outer_sum, ((0, padding), (0, 0)))
    return (
        layer_out,
        frames_grad,
        query_sum,
        querybias_sum,
        key_sum,
        value_sum,
        valuebias_sum,
        output_sum,
        norm_sums[0],
        norm_sums[1],
        norm_sums[2],
        inner_full,
        innerbias_full,
        outer_full,
        norm_sums[3],
        norm_sums[4],
        norm_sums[5],
    )


def solution(mesh):
    in_specs = (
        P("rows", None, None),
        P("rows", None),
        P("rows", None, None),
        P(None, "heads"),
        P("heads"),
        P(None, "heads"),
        P(None, "heads"),
        P("heads"),
        P("heads", None),
        P(),
        P(),
        P(),
        P(None, "heads"),
        P("heads"),
        P("heads", None),
        P(),
        P(),
        P(),
    )
    out_specs = (
        P("rows", None, None),
        P("rows", None, None),
        P(None, "heads"),
        P("heads"),
        P(None, "heads"),
        P(None, "heads"),
        P("heads"),
        P("heads", None),
        P(),
        P(),
        P(),
        P(None, "heads"),
        P("heads"),
        P("heads", None),
        P(),
        P(),
        P(),
    )
    return jax.shard_map(
        per_device, mesh=mesh, in_specs=in_specs, out_specs=out_specs, check_vma=False
    )
```

profile of v0, /device:TPU:0, one launch (start us, length us, event | category | flops | bytes accessed | tf_op | source)
XLA Modules:
  0.0 859.3 jit_solution(14711500250248380439)
XLA Ops:
  12.1 4.2 reshape.251
  39.2 28.9 %while.26 = (s32[]{:T(128)}, bf16[3,800,3,64]{1,3,2,0:T(8,128)(2,1)}, f32[3,3,800,1]{2,1,3,0:T(4,128)S(1)}, bf16[3,800,3,64]{1,3,2,0:T(8,128)(2,1)}, s32[3,800]{...) while((s32[]{:T(128)}, ...), condition=%wide.region_3.4_spmd, body=%wide.region_0.3_spmd.sunk | while | flops 513431200 | bytes 27083748 | solution.py:154
  44.6 4.2 fusion.144
  54.3 4.2 fusion.144
  63.9 4.2 fusion.144
  73.8 68.6 %all-reduce.16.cloned.1.call-done = bf16[3,800,640]{2,1,0:T(8,128)(2,1)} async-done(((bf16[3,800,640]{2,1,0:T(8,128)(2,1)}), bf16[3,800,640]{2,1,0:T(8,128)(2,1)}) %all-reduce.16.cloned.1.call-update) | async-done | bytes 3072016
  148.1 28.3 %all-gather.6.cloned.1.call-done = bf16[3,800,640]{2,1,0:T(8,128)(2,1)} async-done(((bf16[3,200,640]{2,1,0:T(8,128)(2,1)}), bf16[3,800,640]{2,1,0:T(8,128)(2,1)}) %all-gather.6.cloned.1.call-update) | async-done | bytes 3072016 | tf_op jit(solution)/shard_map/all_gather | solution.py:128
  176.4 21.5 %multiply_convert_fusion.1 = (bf16[2400,672]{0,1:T(8,128)(2,1)S(1)}, f32[2400,672]{0,1:T(8,128)}, f32[2400,672]{0,1:T(8,128)}) fusion(f32[672]{0:T(1024)S(1)} %bitcast.190, bf16[2400,640]{1,0:T(8,128)(2,1)} %bitcast.186, bf16[640,768]{1,0:T(8,128)(2,1)} %param.34), kind=kOutput, calls=%fused_computation.71 | convolution fusion | flops 2170828800 | bytes 20185728 | tf_op jit(solution)/shard_map/dot_general | solution.py:165
  197.9 4.9 convolution_convert_fusion.1
  202.9 67.3 %all-reduce.18.cloned.1.call-done = bf16[3,800,640]{2,1,0:T(8,128)(2,1)} async-done(((bf16[3,800,640]{2,1,0:T(8,128)(2,1)}), bf16[3,800,640]{2,1,0:T(8,128)(2,1)}) %all-reduce.18.cloned.1.call-update) | async-done | bytes 3072016
  277.2 27.9 %all-gather.10.cloned.1.call-done = bf16[3,800,640]{2,1,0:T(8,128)(2,1)} async-done(((bf16[3,200,640]{2,1,0:T(8,128)(2,1)}), bf16[3,800,640]{2,1,0:T(8,128)(2,1)}) %all-gather.10.cloned.1.call-update) | async-done | bytes 3072016 | tf_op jit(solution)/shard_map/all_gather | solution.py:128
  305.1 11.2 %convert_reduce_fusion = (f32[672]{0:T(1024)}, bf16[2400,672]{0,1:T(8,128)(2,1)S(1)}) fusion(f32[2400,672]{0,1:T(8,128)} %get-tuple-element.282, bf16[2400,640]{1,0:T(8,128)(2,1)} %bitcast.188, bf16[768,640]{1,0:T(8,128)(2,1)} %param.36, bf16[672]{0:T(1024)(128)(2,1)S(1)} %fusion.85, f32[2400,672]{0,1:T(8,128)} %get-tuple-element.289, f32[672]{0:T(1024)S(1)} %bitcast.191), kind=kOutput, calls=%fused_computation.69 | convolution fusion | flops 2092231040 | bytes 20238912 | tf_op jit(solution)/shard_map/td,cd->tc/dot_general | solution.py:188
  316.3 4.8 convolution_convert_fusion
  321.2 67.4 %all-reduce.20.cloned.1.call-done = bf16[3,800,640]{2,1,0:T(8,128)(2,1)} async-done(((bf16[3,800,640]{2,1,0:T(8,128)(2,1)}), bf16[3,800,640]{2,1,0:T(8,128)(2,1)}) %all-reduce.20.cloned.1.call-update) | async-done | bytes 3072016
  396.7 28.3 %all-gather.12.cloned.1.call-done = bf16[3,800,640]{2,1,0:T(8,128)(2,1)} async-done(((bf16[3,200,640]{2,1,0:T(8,128)(2,1)}), bf16[3,800,640]{2,1,0:T(8,128)(2,1)}) %all-gather.12.cloned.1.call-update) | async-done | bytes 3072016 | tf_op jit(solution)/shard_map/all_gather | solution.py:128
  429.0 4.2 reshape.256
  439.0 54.1 %while.27 = (s32[]{:T(128)}, bf16[3,800,3,64]{1,3,2,0:T(8,128)(2,1)}, bf16[3,800,3,64]{1,3,2,0:T(8,128)(2,1)}, bf16[3,800,3,64]{1,3,2,0:T(8,128)(2,1)}, bf16[3,8...) while((s32[]{:T(128)}, ...), condition=%wide.region_17.18_spmd, body=%wide.region_15.17_spmd.sunk | while | flops 1259005568 | bytes 69375384 | solution.py:210
  528.7 7.0 fusion.94
  547.3 40.9 %all-reduce.22.cloned.1.call-done = bf16[3,800,640]{2,1,0:T(8,128)(2,1)} async-done(((bf16[3,800,640]{2,1,0:T(8,128)(2,1)}), bf16[3,800,640]{2,1,0:T(8,128)(2,1)}) %all-reduce.22.cloned.1.call-update) | async-done | bytes 3072016
  590.3 27.6 %all-gather.8.cloned.1.call-done = bf16[3,800,640]{2,1,0:T(8,128)(2,1)} async-done(((bf16[3,200,640]{2,1,0:T(8,128)(2,1)}), bf16[3,800,640]{2,1,0:T(8,128)(2,1)}) %all-gather.8.cloned.1.call-update) | async-done | bytes 3072016 | tf_op jit(solution)/shard_map/all_gather | solution.py:128
  618.0 45.5 %all-reduce.7 = (f32[640]{0:T(1024)}, f32[640]{0:T(1024)}, f32[640]{0:T(1024)}, f32[640]{0:T(1024)}, f32[640]{0:T(1024)}, /*index=5*/f32[640]{0:T(1024)}) all-reduce(f32[640]{0:T(1024)S(1)} %get-tuple-element.276, f32[640]{0:T(1024)S(1)} %get-tuple-element.216, ...), channel_id=1, replica_groups=mesh['rows'=8,'heads'=4] {'rows','heads'}, use_global_device_ids=true, to_apply=%region_28.29 | all-reduce | flops 3840 | bytes 30720 | tf_op jit(solution)/shard_map/psum | solution.py:241
  665.4 23.1 %all-reduce.8 = (f32[192]{0:T(256)}, f32[192]{0:T(256)}, f32[672]{0:T(1024)S(1)}) all-reduce(f32[192]{0:T(256)S(1)} %reduce_sum.184, f32[192]{0:T(256)S(1)} %reduce_sum.186, f32[672]{0:T(1024)S(1)} %copy-done.32), channel_id=1, replica_groups=mesh['rows'=8,'heads'=4] {'rows'}, use_global_device_ids=true, to_apply=%region_21.22 | all-reduce | flops 1056 | bytes 8448 | tf_op jit(solution)/shard_map/psum | solution.py:262
  689.0 126.2 %all-reduce.24.cloned.1.call-done = (f32[640,192]{0,1:T(8,128)}, f32[640,192]{0,1:T(8,128)}, f32[640,192]{0,1:T(8,128)}, f32[192,640]{1,0:T(8,128)}, f32[640,672]{0,1:T(8,128)}, /*index=5*/f32[672,640]{1,0:T(8,128)}) async-done(((f32[640,192]{0,1:T(8,128)}, f32[640,192]{0,1:T(8,128)}, f32[640,192]{0,1:T(8,128)}, f32[192,640]{1,0:T(8,128)}, f32[640,672]{0,1:T(8,128)}, /*index=5*/f32[672,640]{1,0:T(8,128)}), ...) | async-done | bytes 5406736 | tf_op jit(solution)/shard_map/psum | solution.py:262
  820.7 23.5 %all-gather.14.cloned.1.call-done = bf16[3,800,640]{2,1,0:T(8,128)(2,1)} async-done(((bf16[3,200,640]{2,1,0:T(8,128)(2,1)}), bf16[3,800,640]{2,1,0:T(8,128)(2,1)}) %all-gather.14.cloned.1.call-update) | async-done | bytes 3072016 | tf_op jit(solution)/shard_map/all_gather | solution.py:128
  (224 shorter events, 198.4 us)
Async XLA Ops:
  7.2 135.2 %all-reduce.16.cloned.1.call-start = ((), (), s32[]{:S(2)}) async-start(), calls=%async_computation.5 | async-start | bytes 6144000
  68.1 74.4 %copy-start.24 = (f32[640]{0:T(1024)S(1)}, f32[640]{0:T(1024)}, u32[]{:S(2)}) copy-start(f32[640]{0:T(1024)} %param.31) | copy-start | bytes 7684
  72.2 73.3 %copy-start.26 = (f32[640]{0:T(1024)S(1)}, f32[640]{0:T(1024)}, u32[]{:S(2)}) copy-start(f32[640]{0:T(1024)} %param.32) | copy-start | bytes 7684
  72.2 73.3 %copy-start.29 = (f32[640]{0:T(1024)S(1)}, f32[640]{0:T(1024)}, u32[]{:S(2)}) copy-start(f32[640]{0:T(1024)} %param.33) | copy-start | bytes 7684
  72.2 104.1 %all-gather.6.cloned.1.call-start = ((), (), s32[]{:S(2)}) async-start(), calls=%async_computation | async-start | bytes 3840000 | tf_op jit(solution)/shard_map/all_gather | solution.py:128
  73.8 102.6 %copy-start.38 = (f32[768]{0:T(1024)S(1)}, f32[768]{0:T(1024)}, u32[]{:S(2)}) copy-start(f32[768]{0:T(1024)} %param.35) | copy-start | bytes 9220
  148.0 122.2 %all-reduce.18.cloned.1.call-start = ((), (), s32[]{:S(2)}) async-start(), calls=%async_computation.6 | async-start | bytes 6144000
  202.7 67.5 %copy-start.33 = (f32[640]{0:T(1024)S(1)}, f32[640]{0:T(1024)}, u32[]{:S(2)}) copy-start(f32[640]{0:T(1024)} %param.37) | copy-start | bytes 7684
  202.8 70.1 %copy-start.27 = (f32[640]{0:T(1024)S(1)}, f32[640]{0:T(1024)}, u32[]{:S(2)}) copy-start(f32[640]{0:T(1024)} %param.38) | copy-start | bytes 7684
  202.8 102.3 %all-gather.10.cloned.1.call-start = ((), (), s32[]{:S(2)}) async-start(), calls=%async_computation.2 | async-start | bytes 3840000 | tf_op jit(solution)/shard_map/all_gather | solution.py:128
  202.9 71.3 %copy-start.34 = (f32[640]{0:T(1024)S(1)}, f32[640]{0:T(1024)}, u32[]{:S(2)}) copy-start(f32[640]{0:T(1024)} %param.39) | copy-start | bytes 7684
  276.7 111.9 %all-reduce.20.cloned.1.call-start = ((), (), s32[]{:S(2)}) async-start(), calls=%async_computation.7 | async-start | bytes 6144000
  321.2 103.8 %all-gather.12.cloned.1.call-start = ((), (), s32[]{:S(2)}) async-start(), calls=%async_computation.3 | async-start | bytes 3840000 | tf_op jit(solution)/shard_map/all_gather | solution.py:128
  396.6 191.6 %all-reduce.22.cloned.1.call-start = ((), (), s32[]{:S(2)}) async-start(), calls=%async_computation.8 | async-start | bytes 6144000
  520.7 97.3 %all-gather.8.cloned.1.call-start = ((), (), s32[]{:S(2)}) async-start(), calls=%async_computation.1 | async-start | bytes 3840000 | tf_op jit(solution)/shard_map/all_gather | solution.py:128
  521.4 293.8 %all-reduce.24.cloned.1.call-start = ((), (), s32[]{:S(2)}) async-start(), calls=%async_computation.9 | async-start | bytes 10813440 | tf_op jit(solution)/shard_map/psum | solution.py:262
  547.2 41.0 %copy-start.4 = (f32[3,200,640]{2,1,0:T(8,128)S(1)}, f32[3,200,640]{2,1,0:T(8,128)}, u32[]{:S(2)}) copy-start(f32[3,200,640]{2,1,0:T(8,128)} %copy-done.3) | copy-start | bytes 4608004
  547.2 70.8 %copy-start.28 = (f32[640]{0:T(1024)S(1)}, f32[640]{0:T(1024)}, u32[]{:S(2)}) copy-start(f32[640]{0:T(1024)} %get-tuple-element.222) | copy-start | bytes 7684
  547.2 70.8 %copy-start.30 = (f32[640]{0:T(1024)S(1)}, f32[640]{0:T(1024)}, u32[]{:S(2)}) copy-start(f32[640]{0:T(1024)} %get-tuple-element.218) | copy-start | bytes 7684
  547.2 70.7 %copy-start.31 = (f32[640]{0:T(1024)S(1)}, f32[640]{0:T(1024)}, u32[]{:S(2)}) copy-start(f32[640]{0:T(1024)} %get-tuple-element.219) | copy-start | bytes 7684
  547.2 116.2 %copy-start.8 = (bf16[3,800,3,64]{1,3,2,0:T(8,128)(2,1)S(1)}, bf16[3,800,3,64]{1,3,2,0:T(8,128)(2,1)}, u32[]{:S(2)}) copy-start(bf16[3,800,3,64]{1,3,2,0:T(8,128)(2,1)} %get-tuple-element.113) | copy-start | bytes 2764804
  547.2 118.1 %copy-start.32 = (f32[672]{0:T(1024)S(1)}, f32[672]{0:T(1024)}, u32[]{:S(2)}) copy-start(f32[672]{0:T(1024)} %get-tuple-element.290) | copy-start | bytes 8068
  547.3 297.0 %all-gather.14.cloned.1.call-start = ((), (), s32[]{:S(2)}) async-start(), calls=%async_computation.4 | async-start | bytes 3840000 | tf_op jit(solution)/shard_map/all_gather | solution.py:128
  818.6 25.7 %copy-start.14 = (bf16[3,800,640]{2,1,0:T(8,128)(2,1)S(1)}, bf16[3,800,640]{2,1,0:T(8,128)(2,1)}, u32[]{:S(2)}) copy-start(bf16[3,800,640]{2,1,0:T(8,128)(2,1)} %all-gather.8.cloned.1.call-done) | copy-start | bytes 9216004
  (32 other events, 133.7 us)
Sparse Core Ops, SparseCore 0:
  72.4 70.0 all-reduce.15
  148.1 28.2 all-gather.5
  202.9 67.3 all-reduce.17
  276.9 28.1 all-gather.9
  321.3 67.3 all-reduce.19
  396.7 28.1 all-gather.11
  520.8 67.3 all-reduce.21
  589.7 28.1 all-gather.7
  623.6 191.6 all-reduce.23
  817.3 26.8 all-gather.13
where the time goes:
time: 870 us; the launch traced here: 859 us
  waiting for transfers between devices  507 us (58%)
  matrix products  151 us (17%)
  local copies, waits for them, and re-layouts  76.6 us (9%)
  blocking collectives  68.6 us (8%)
  other arithmetic  38.9 us (4%)
  between operations  15.6 us (2%)
    unnamed x14, waiting for transfers between devices  245 us
    all_gather x5, waiting for transfers between devices, spread(): return lax.all_gather(value, 'heads', axis=1, tiled=True)  136 us
    psum x1, waiting for transfers between devices, per_device(): lax.psum((query_part, querybias_part, key_part, value_part, valuebias_par...  126 us
    psum x1, blocking collectives, per_device(): lax.psum((outputbias_part, firstgain_part, firstshift_part, outerbias_par...  45.5 us
    psum x1, blocking collectives, per_device(): lax.psum((query_part, querybias_part, key_part, value_part, valuebias_par...  23.1 us
    dot_general x1, matrix products, per_device(): jnp.dot(normed_low, up_weight, preferred_element_type=jnp.float32) + up_bias  21.5 us
  transfers between devices with their start and end apart: 10, of which 10 were waited for; matrix products, arithmetic and copies ran while one was open for 4% of the time, Pallas kernels for 0%

commit v1 on v0

v1 whole, which is shorter than its diff:
```python
import math

import jax
import jax.numpy as jnp
from jax import lax
from jax.experimental import pallas as pl
from jax.experimental.pallas import tpu as pltpu
from jax.sharding import PartitionSpec as P

HEADS_LIVE = 10
HEAD_DIM = 64
FF_LIVE = 2240
PAD_HEAD = 128
SEGMENTS = 5
MASK_STEP = -(2.0**30)
norm_eps = 1e-05
f32 = jnp.float32
bf16 = jnp.bfloat16


def dot(a, b, ca, cb):
    return lax.dot_general(a, b, (((ca,), (cb,)), ((), ())), preferred_element_type=f32)


def three_parts(value):
    high = value.astype(bf16).astype(f32)
    middle = (value - high).astype(bf16).astype(f32)
    return high, middle, value - high - middle


def feature_rows(base, value):
    high, middle, low = three_parts(-value)
    row = lax.broadcasted_iota(jnp.int32, base.shape, 0)
    base = jnp.where(row == SEGMENTS, high, base)
    base = jnp.where(row == SEGMENTS + 1, middle, base)
    return jnp.where(row == SEGMENTS + 2, low, base).astype(bf16)


def attend_kernel(
    place, block_ref, row_ref, qkv_ref, out_ref, qbias_ref, vbias_ref, keyf_ref, queryf_ref,
    sum_ref, total_ref, query_ref, key_ref, value_ref, context_ref,
):
    step = pl.program_id(0)
    per_row, live = place[1], place[2]
    row_now = (place[0] + step) // per_row
    row_before = (place[0] + step - 1) // per_row
    length = row_ref.shape[1]
    width = qbias_ref.shape[0]
    heads = width // HEAD_DIM

    @pl.when(jnp.logical_or(step == 0, row_now != row_before))
    def _():
        frames = row_ref[0]
        keys = dot(frames, qkv_ref[width : 2 * width], 1, 1).astype(bf16)
        values = (dot(frames, qkv_ref[2 * width : 3 * width], 1, 1) + vbias_ref[...]).astype(bf16)
        features = keyf_ref[0]
        for head in range(heads):
            cut = slice(head * HEAD_DIM, (head + 1) * HEAD_DIM)
            key_ref[0, head * length : (head + 1) * length] = jnp.concatenate(
                [keys[:, cut], features], axis=1
            )
            value_ref[0, head * length : (head + 1) * length] = jnp.concatenate(
                [values[:, cut], features], axis=1
            )

    queries = (dot(qkv_ref[0:width], block_ref[0], 1, 1) + qbias_ref[...]).astype(bf16)
    queries = queries * jnp.asarray(HEAD_DIM**-0.5, bf16)
    for head in range(heads):
        query_ref[0, head * PAD_HEAD : head * PAD_HEAD + HEAD_DIM] = queries[
            head * HEAD_DIM : (head + 1) * HEAD_DIM
        ]
        query_ref[0, head * PAD_HEAD + HEAD_DIM : (head + 1) * PAD_HEAD] = queryf_ref[0]
    context_ref[...] = jnp.zeros_like(context_ref)

    def one_head(head, carry):
        keys = key_ref[0, pl.ds(pl.multiple_of(head * length, 16), length)]
        values = value_ref[0, pl.ds(pl.multiple_of(head * length, 16), length)]
        start = pl.multiple_of(head * PAD_HEAD, PAD_HEAD)
        scores = dot(keys, query_ref[0, pl.ds(start, PAD_HEAD)], 1, 0)
        highest = jnp.max(scores, axis=0, keepdims=True)
        probs = jnp.exp(scores - highest).astype(bf16)
        mixed = dot(values, probs, 0, 0)
        total = mixed[HEAD_DIM + SEGMENTS : HEAD_DIM + SEGMENTS + 1]
        context = mixed[0:HEAD_DIM] / total
        context_ref[0, pl.ds(pl.multiple_of(head * HEAD_DIM, HEAD_DIM), HEAD_DIM)] = context.astype(bf16)
        base = queryf_ref[0, 0:16].astype(f32)
        query_ref[0, pl.ds(start + HEAD_DIM, 16)] = feature_rows(base, highest + jnp.log(total))
        return carry

    lax.fori_loop(0, live, one_head, 0)
    total_ref[0] = sum_ref[0] + dot(context_ref[0], out_ref[...], 0, 0)


def attend_back_kernel(
    place, block_ref, row_ref, qkv_ref, out_ref, query_ref, key_ref, value_ref, context_ref,
    grad_ref, blocksum_ref, rowsum_ref,
    gradw_ref, qbias_ref, vbias_ref, blockout_ref, rowout_ref,
    weight_acc, dkey, dvalue, picked, dcontext, dquery,
):
    step = pl.program_id(0)
    steps = pl.num_programs(0)
    per_row, live = place[1], place[2]
    row_now = (place[0] + step) // per_row
    row_before = (place[0] + step - 1) // per_row
    row_after = (place[0] + step + 1) // per_row
    length = row_ref.shape[1]
    width = qbias_ref.shape[0]
    heads = width // HEAD_DIM

    @pl.when(step == 0)
    def _():
        weight_acc[...] = jnp.zeros_like(weight_acc)
        qbias_ref[...] = jnp.zeros_like(qbias_ref)
        vbias_ref[...] = jnp.zeros_like(vbias_ref)
        picked[...] = jnp.zeros_like(picked)

    @pl.when(jnp.logical_or(step == 0, row_now != row_before))
    def _():
        dkey[...] = jnp.zeros_like(dkey)
        dvalue[...] = jnp.zeros_like(dvalue)

    dcontext[...] = dot(out_ref[...], grad_ref[0], 1, 1).astype(bf16)
    dquery[...] = jnp.zeros_like(dquery)

    def one_head(head, carry):
        own = pl.ds(pl.multiple_of(head * HEAD_DIM, HEAD_DIM), HEAD_DIM)
        keys = key_ref[0, pl.ds(pl.multiple_of(head * length, 16), length)]
        values = value_ref[0, pl.ds(pl.multiple_of(head * length, 16), length)]
        queries = query_ref[0, pl.ds(pl.multiple_of(head * PAD_HEAD, PAD_HEAD), PAD_HEAD)]
        grad = dcontext[own]
        inner = jnp.sum(grad.astype(f32) * context_ref[0, own].astype(f32), axis=0, keepdims=True)
        extra = feature_rows(jnp.zeros((PAD_HEAD - HEAD_DIM, grad.shape[1]), f32), inner)
        probs = jnp.exp(dot(keys, queries, 1, 0))
        dprobs = dot(values, jnp.concatenate([grad, extra], axis=0), 1, 0)
        dscores = (probs * dprobs).astype(bf16)
        picked[0, pl.ds(pl.multiple_of(head * width + head * HEAD_DIM, HEAD_DIM), HEAD_DIM)] = grad
        picked[1, pl.ds(pl.multiple_of(head * width + head * HEAD_DIM, HEAD_DIM), HEAD_DIM)] = queries[0:HEAD_DIM]
        place_head = pl.ds(pl.multiple_of(head * width, HEAD_DIM), width)
        dvalue[...] += dot(probs.astype(bf16), picked[0, place_head], 1, 1)
        dkey[...] += dot(dscores, picked[1, place_head], 1, 1)
        dquery[own] = (dot(keys, dscores, 0, 0)[0:HEAD_DIM] * HEAD_DIM**-0.5).astype(bf16)
        return carry

    lax.fori_loop(0, live, one_head, 0)
    weight_acc[0:width] += dot(dquery[...], block_ref[0], 1, 0)
    weight_acc[3 * width :] += dot(context_ref[0], grad_ref[0], 1, 0)
    blockout_ref[0] = blocksum_ref[0] + dot(dquery[...], qkv_ref[0:width], 0, 0)
    qbias_ref[...] += jnp.sum(dquery[...].astype(f32), axis=1, keepdims=True)

    @pl.when(jnp.logical_or(step == steps - 1, row_now != row_after))
    def _():
        keys_low = dkey[...].astype(bf16)
        values_low = dvalue[...].astype(bf16)
        weight_acc[width : 2 * width] += dot(keys_low, row_ref[0], 0, 0)
        weight_acc[2 * width : 3 * width] += dot(values_low, row_ref[0], 0, 0)
        rowout_ref[0] = (
            rowsum_ref[0]
            + dot(keys_low, qkv_ref[width : 2 * width], 1, 0)
            + dot(values_low, qkv_ref[2 * width : 3 * width], 1, 0)
        )
        vbias_ref[...] += jnp.sum(values_low.astype(f32), axis=0, keepdims=True)

    @pl.when(step == steps - 1)
    def _():
        gradw_ref[...] = weight_acc[...].astype(bf16)


def whole(shape):
    return pl.BlockSpec(shape, lambda b, place: (0,) * len(shape))


def attend(place, blocks, rows, qkv, out, qbias, vbias, keyf, queryf, partial):
    steps, size, depth = partial.shape
    count, length, _ = rows.shape
    width = qbias.shape[0]
    heads = width // HEAD_DIM
    window = min(2, count)
    row_of = lambda b, place: ((place[0] + b) // place[1], 0, 0)
    rel_row = lambda b, place: ((place[0] + b) // place[1] - place[0] // place[1], 0, 0)
    block_of = lambda b, place: (place[0] + b, 0, 0)
    local = lambda b, place: (b, 0, 0)
    spec = pltpu.PrefetchScalarGridSpec(
        num_scalar_prefetch=1,
        grid=(steps,),
        in_specs=[
            pl.BlockSpec((1, size, depth), block_of),
            pl.BlockSpec((1, length, depth), row_of),
            whole(qkv.shape),
            whole(out.shape),
            whole(qbias.shape),
            whole(vbias.shape),
            pl.BlockSpec((1,) + keyf.shape[1:], row_of),
            pl.BlockSpec((1,) + queryf.shape[1:], block_of),
            pl.BlockSpec((1, size, depth), local),
        ],
        out_specs=[
            pl.BlockSpec((1, size, depth), local),
            pl.BlockSpec((1, heads * PAD_HEAD, size), local),
            pl.BlockSpec((1, heads * length, PAD_HEAD), rel_row),
            pl.BlockSpec((1, heads * length, PAD_HEAD), rel_row),
            pl.BlockSpec((1, width, size), local),
        ],
    )
    return pl.pallas_call(
        attend_kernel,
        grid_spec=spec,
        out_shape=[
            jax.ShapeDtypeStruct(partial.shape, f32),
            jax.ShapeDtypeStruct((steps, heads * PAD_HEAD, size), bf16),
            jax.ShapeDtypeStruct((window, heads * length, PAD_HEAD), bf16),
            jax.ShapeDtypeStruct((window, heads * length, PAD_HEAD), bf16),
            jax.ShapeDtypeStruct((steps, width, size), bf16),
        ],
        cost_estimate=pl.CostEstimate(
            flops=8 * steps * size * length * width, bytes_accessed=2**23, transcendentals=0
        ),
        name="attend",
    )(place, blocks, rows, qkv, out, qbias, vbias, keyf, queryf, partial)


def attend_back(place, blocks, rows, qkv, out, saved, grad, blocksum, rowsum):
    query, key, value, context = saved
    steps, size, depth = blocksum.shape
    count, length, _ = rows.shape
    width = out.shape[0]
    heads = width // HEAD_DIM
    row_of = lambda b, place: ((place[0] + b) // place[1], 0, 0)
    rel_row = lambda b, place: ((place[0] + b) // place[1] - place[0] // place[1], 0, 0)
    block_of = lambda b, place: (place[0] + b, 0, 0)
    local = lambda b, place: (b, 0, 0)
    spec = pltpu.PrefetchScalarGridSpec(
        num_scalar_prefetch=1,
        grid=(steps,),
        in_specs=[
            pl.BlockSpec((1, size, depth), block_of),
            pl.BlockSpec((1, length, depth), row_of),
            whole(qkv.shape),
            whole(out.shape),
            pl.BlockSpec((1,) + query.shape[1:], local),
            pl.BlockSpec((1,) + key.shape[1:], rel_row),
            pl.BlockSpec((1,) + value.shape[1:], rel_row),
            pl.BlockSpec((1,) + context.shape[1:], local),
            pl.BlockSpec((1, size, depth), local),
            pl.BlockSpec((1, size, depth), local),
            pl.BlockSpec((1, length, depth), rel_row),
        ],
        out_specs=[
            whole((4 * width, depth)),
            whole((width, 1)),
            whole((1, width)),
            pl.BlockSpec((1, size, depth), local),
            pl.BlockSpec((1, length, depth), rel_row),
        ],
        scratch_shapes=[
            pltpu.VMEM((4 * width, depth), f32),
            pltpu.VMEM((length, width), f32),
            pltpu.VMEM((length, width), f32),
            pltpu.VMEM((2, heads * width, size), bf16),
            pltpu.VMEM((width, size), bf16),
            pltpu.VMEM((width, size), bf16),
        ],
    )
    return pl.pallas_call(
        attend_back_kernel,
        grid_spec=spec,
        out_shape=[
            jax.ShapeDtypeStruct((4 * width, depth), bf16),
            jax.ShapeDtypeStruct((width, 1), f32),
            jax.ShapeDtypeStruct((1, width), f32),
            jax.ShapeDtypeStruct(blocksum.shape, f32),
            jax.ShapeDtypeStruct(rowsum.shape, f32),
        ],
        input_output_aliases={11: 4},
        cost_estimate=pl.CostEstimate(
            flops=20 * steps * size * length * width, bytes_accessed=2**23, transcendentals=0
        ),
        name="attend_back",
    )(place, blocks, rows, qkv, out, query, key, value, context, grad, blocksum, rowsum)


def swap(value, axis, distance):
    size = lax.axis_size(axis)
    return lax.ppermute(value, axis, [(i, i ^ distance) for i in range(size)])


def add_low(a, b):
    return (a.astype(f32) + b.astype(f32)).astype(bf16)


def sum_slots(parts):
    parts = list(parts)
    distance = 1
    while distance < len(parts):
        for slot in range(0, len(parts), 2 * distance):
            arrived = swap(parts[slot + distance], "heads", distance)
            parts[slot] = add_low(parts[slot], arrived) if arrived.dtype == bf16 else parts[slot] + arrived
        distance *= 2
    return parts[0]


def sum_rows(value):
    size = lax.axis_size("rows")
    here = lax.axis_index("rows")
    taken = []
    distance = 1
    while distance < size:
        half = value.shape[0] // 2
        if value.shape[0] % 2 == 0 and half % 8 == 0 and value.dtype == bf16:
            upper = (here // distance) % 2 == 1
            low_part, high_part = value[:half], value[half:]
            sent = swap(jnp.where(upper, low_part, high_part), "rows", distance)
            value = add_low(jnp.where(upper, high_part, low_part), sent)
            taken.append(distance)
        else:
            arrived = swap(value, "rows", distance)
            value = add_low(value, arrived) if value.dtype == bf16 else value + arrived
        distance *= 2
    for distance in reversed(taken):
        upper = (here // distance) % 2 == 1
        arrived = swap(value, "rows", distance)
        value = jnp.concatenate(
            [jnp.where(upper, arrived, value), jnp.where(upper, value, arrived)], axis=0
        )
    return value


def sum_heads(value):
    distance = 1
    while distance < lax.axis_size("heads"):
        value = value + swap(value, "heads", distance)
        distance *= 2
    return value


def gather_slots(value):
    slots = [value]
    distance = 1
    group = lax.axis_size("heads")
    slots = {0: value}
    distance = group // 2
    while distance >= 1:
        for slot in list(slots):
            slots[slot ^ distance] = swap(slots[slot], "heads", distance)
        distance //= 2
    return [slots[j] for j in range(group)]


def gather_frames(own, full_shape):
    position = lax.axis_index("heads")
    size = own.shape[0]
    result = jnp.zeros((full_shape[0] * full_shape[1], full_shape[2]), own.dtype)
    for slot, piece in enumerate(gather_slots(own)):
        result = lax.dynamic_update_slice(result, piece, ((position ^ slot) * size, 0))
    return result.reshape(full_shape)


def layer_stats(value):
    centre = value - jnp.mean(value, axis=-1, keepdims=True)
    inverse = lax.rsqrt(jnp.mean(centre * centre, axis=-1, keepdims=True) + norm_eps)
    return (centre * inverse, inverse)


def norm_back(grad_out, normal, inverse, gain):
    scaled = grad_out * gain
    return inverse * (
        scaled
        - jnp.mean(scaled, axis=-1, keepdims=True)
        - normal * jnp.mean(scaled * normal, axis=-1, keepdims=True)
    )


def exact_gelu(value):
    return jax.nn.gelu(value, approximate=False)


def per_device(
    frames, segment_ids, cotangent, query_weight, query_bias, key_weight, value_weight, value_bias,
    output_weight, output_bias, first_gain, first_shift, inner_weight, inner_bias, outer_weight,
    outer_bias, second_gain, second_shift,
):
    group = lax.axis_size("heads")
    position = lax.axis_index("heads")
    row_count, row_length, depth = frames.shape
    own_len = row_count * row_length // group
    size = math.gcd(row_length, own_len)
    steps = own_len // size
    per_row = row_length // size
    width = query_weight.shape[1]
    heads_here = width // HEAD_DIM
    per_head = FF_LIVE // HEADS_LIVE
    hidden_slots = inner_weight.shape[1]
    hidden_cap = min(hidden_slots, (HEADS_LIVE + group - 1) // group * per_head)

    def live_of(index):
        return HEADS_LIVE // group + (index < HEADS_LIVE % group).astype(jnp.int32)

    live_heads = live_of(position)
    head_mask = (jnp.arange(width, dtype=jnp.int32) // HEAD_DIM < live_heads)[:, None]
    hidden_mask = (jnp.arange(hidden_cap, dtype=jnp.int32) < live_heads * per_head)[:, None]
    qkv_own = jnp.concatenate([query_weight.T, key_weight.T, value_weight.T], axis=0)
    out_own = jnp.where(head_mask, output_weight, 0)
    up_own = inner_weight.T[:hidden_cap]
    down_own = jnp.where(hidden_mask, outer_weight[:hidden_cap], 0)
    bias_own = jnp.concatenate([query_bias, value_bias, inner_bias[:hidden_cap]])[None]

    qkv = gather_slots(qkv_own)
    out = gather_slots(out_own)
    bias = gather_slots(bias_own)
    up = gather_slots(up_own)
    down = gather_slots(down_own)

    blocks = frames.reshape(row_count * per_row, size, depth)
    kinds = jnp.arange(-1, SEGMENTS - 1, dtype=jnp.int32)
    same = segment_ids[:, :, None] == kinds
    keyf = jnp.concatenate(
        [
            same.astype(bf16),
            jnp.ones((row_count, row_length, 3), bf16),
            jnp.zeros((row_count, row_length, HEAD_DIM - SEGMENTS - 3), bf16),
        ],
        axis=2,
    )
    ids_blocks = segment_ids.reshape(row_count * per_row, 1, size)
    queryf = jnp.where(ids_blocks == kinds[:, None], 0.0, MASK_STEP).astype(bf16)
    queryf = jnp.pad(queryf, ((0, 0), (0, HEAD_DIM - SEGMENTS), (0, 0)))

    def own_part(value):
        flat = value.reshape((row_count * row_length,) + value.shape[2:])
        return lax.dynamic_slice_in_dim(flat, position * own_len, own_len, 0)

    places = [
        jnp.stack([position * steps, jnp.int32(per_row), live_of(position ^ slot)])
        for slot in range(group)
    ]
    total = jnp.zeros((steps, size, depth), f32)
    saved = []
    for slot in range(group):
        qbias = bias[slot][0, :width, None]
        vbias = bias[slot][:, width : 2 * width]
        total, *kept = attend(
            places[slot], blocks, frames, qkv[slot], out[slot], qbias, vbias, keyf, queryf, total
        )
        saved.append(kept)
    attended = total.reshape(own_len, depth)

    hidden_one = own_part(frames).astype(f32) + attended + output_bias
    normal_one, inverse_one = layer_stats(hidden_one)
    normed_one = normal_one * first_gain + first_shift
    normed_low = normed_one.astype(bf16)
    actives, pulls = [], []
    ffn = 0.0
    for slot in range(group):
        inner_pre = dot(normed_low, up[slot], 1, 1) + bias[slot][:, 2 * width :]
        active, pull = jax.vjp(exact_gelu, inner_pre)
        actives.append(active.astype(bf16))
        pulls.append(pull)
        ffn = ffn + dot(actives[-1], down[slot], 1, 0)
    hidden_two = normed_one + ffn + outer_bias
    normal_two, inverse_two = layer_stats(hidden_two)
    live_rows = (own_part(segment_ids) >= 0).astype(f32)[:, None]
    final_out = (normal_two * second_gain + second_shift) * live_rows
    layer_out = gather_frames(final_out.astype(bf16), frames.shape)
    grad_final = own_part(cotangent).astype(f32) * live_rows
    secondgain_part = jnp.sum(grad_final * normal_two, axis=0)
    secondshift_part = jnp.sum(grad_final, axis=0)
    grad_hidden_two = norm_back(grad_final, normal_two, inverse_two, second_gain)
    outerbias_part = jnp.sum(grad_hidden_two, axis=0)
    grad_ffn = grad_hidden_two.astype(bf16)

    down_parts, up_parts, innerbias_parts = [], [], []
    grad_normed = grad_hidden_two
    for slot in range(group):
        down_parts.append(dot(actives[slot], grad_ffn, 0, 0).astype(bf16))
        grad_active = dot(grad_ffn, down[slot], 1, 1)
        grad_inner = pulls[slot](grad_active)[0].astype(bf16)
        up_parts.append(dot(grad_inner, normed_low, 0, 0).astype(bf16))
        innerbias_parts.append(jnp.sum(grad_inner, axis=0, dtype=f32))
        grad_normed = grad_normed + dot(grad_inner, up[slot], 1, 0)
    down_sum = sum_rows(sum_slots(down_parts)).astype(f32)
    up_sum = sum_rows(sum_slots(up_parts)).astype(f32)
    innerbias_sum = sum_rows(sum_slots(innerbias_parts))

    firstgain_part = jnp.sum(grad_normed * normal_one, axis=0)
    firstshift_part = jnp.sum(grad_normed, axis=0)
    grad_hidden_one = norm_back(grad_normed, normal_one, inverse_one, first_gain)
    outputbias_part = jnp.sum(grad_hidden_one, axis=0)
    norm_sums = sum_rows(
        sum_heads(
            jnp.stack(
                [
                    outputbias_part, firstgain_part, firstshift_part,
                    outerbias_part, secondgain_part, secondshift_part,
                ]
            )
        )
    )
    grad_attn = grad_hidden_one.astype(bf16).reshape(steps, size, depth)
    block_sum = grad_hidden_one.reshape(steps, size, depth)
    row_sum = jnp.zeros((min(2, row_count), row_length, depth), f32)
    attn_parts, attnbias_parts = [None] * group, [None] * group
    for slot in reversed(range(group)):
        attn_parts[slot], qb, vb, block_sum, row_sum = attend_back(
            places[slot], blocks, frames, qkv[slot], out[slot], saved[slot], grad_attn,
            block_sum, row_sum,
        )
        attnbias_parts[slot] = jnp.concatenate([qb[:, 0], vb[0]])[None]
    attn_sum = sum_rows(sum_slots(attn_parts)).astype(f32)
    attnbias_sum = sum_rows(sum_slots(attnbias_parts))

    first_row = position * steps // per_row
    spread = jnp.zeros((row_count + 1, row_length, depth), f32)
    spread = lax.dynamic_update_slice(spread, row_sum, (first_row, 0, 0))[:row_count]
    pieces = spread.reshape(group, own_len, depth)

    def piece_of(index):
        return lax.dynamic_index_in_dim(pieces, index, 0, keepdims=False)

    own_grad = block_sum.reshape(own_len, depth) + piece_of(position)
    for distance in range(1, group):
        pairs = []
        for i in range(group):
            j = i ^ distance
            rows_i = range(i * steps // per_row, ((i + 1) * steps - 1) // per_row + 1)
            rows_j = range(j * steps // per_row, ((j + 1) * steps - 1) // per_row + 1)
            if set(rows_i) & set(rows_j):
                pairs.append((i, j))
        if pairs:
            sent = piece_of(position ^ distance).astype(bf16)
            own_grad = own_grad + lax.ppermute(sent, "heads", pairs).astype(f32)
    frames_grad = gather_frames(own_grad.astype(bf16), frames.shape)

    padding = hidden_slots - hidden_cap
    inner_full = jnp.pad(up_sum, ((0, padding), (0, 0))).T
    outer_full = jnp.pad(jnp.where(hidden_mask, down_sum, 0), ((0, padding), (0, 0)))
    innerbias_full = jnp.pad(innerbias_sum, ((0, padding),))
    return (
        layer_out,
        frames_grad,
        attn_sum[:width].T,
        attnbias_sum[0, :width],
        attn_sum[width : 2 * width].T,
        attn_sum[2 * width : 3 * width].T,
        attnbias_sum[0, width:],
        attn_sum[3 * width :],
        norm_sums[0],
        norm_sums[1],
        norm_sums[2],
        inner_full,
        innerbias_full,
        outer_full,
        norm_sums[3],
        norm_sums[4],
        norm_sums[5],
    )


def solution(mesh):
    in_specs = (
        P("rows", None, None), P("rows", None), P("rows", None, None), P(None, "heads"), P("heads"),
        P(None, "heads"), P(None, "heads"), P("heads"), P("heads", None), P(), P(), P(),
        P(None, "heads"), P("heads"), P("heads", None), P(), P(), P(),
    )
    out_specs = (
        P("rows", None, None), P("rows", None, None), P(None, "heads"), P("heads"), P(None, "heads"),
        P(None, "heads"), P("heads"), P("heads", None), P(), P(), P(), P(None, "heads"), P("heads"),
        P("heads", None), P(), P(), P(),
    )
    return jax.shard_map(
        per_device, mesh=mesh, in_specs=in_specs, out_specs=out_specs, check_vma=False
    )
```

time: 870 us -> 446 us (0.51)
  waiting for transfers between devices: 507 us -> 156 us
  Pallas kernels: 0 us -> 107 us
  matrix products: 151 us -> 56.6 us
  starting transfers between devices: 1.03 us -> 70.4 us
  blocking collectives: 68.6 us -> 0 us
  local copies, waits for them, and re-layouts: 76.6 us -> 25.9 us
  other arithmetic: 38.9 us -> 20.6 us
  between operations: 15.6 us -> 2.52 us
    unnamed x14 -> x0, waiting for transfers between devices: 245 us -> none
    ppermute x0 -> x65, waiting for transfers between devices: none -> 156 us  [the longest x63 156 us: swap(): return lax.ppermute(value, axis, [(i, i ^ distance) for i in range(size)])]
    all_gather x5 -> x0, waiting for transfers between devices: 136 us -> none  [spread(): return lax.all_gather(value, 'heads', axis=1, tiled=True)]
    psum x1 -> x0, waiting for transfers between devices: 126 us -> none  [per_device(): lax.psum((query_part, querybias_part, key_part, value_part, valuebias_par...]
    pallas_call x0 -> x8, Pallas kernels: none -> 107 us  [the longest x4 60.4 us: attend_back(): pl.pallas_call(attend_back_kernel, grid_spec=spec, out_shape=[jax.ShapeDt...]
    dot_general x39 -> x24, matrix products: 151 us -> 56.6 us  [dot(): lax.dot_general(a, b, (((ca,), (cb,)), ((), ())), preferred_element_type=...]
    ppermute x0 -> x65, starting transfers between devices: none -> 70.4 us  [the longest x63 69.3 us: swap(): return lax.ppermute(value, axis, [(i, i ^ distance) for i in range(size)])]
    psum x2 -> x0, blocking collectives: 68.6 us -> none  [the longest x1 45.5 us: per_device(): lax.psum((outputbias_part, firstgain_part, firstshift_part, outerbias_par...]
  transfers between devices with their start and end apart: 10 -> 65, of which waited for: 10 -> 22; matrix products, arithmetic and copies ran while one was open for 4% -> 20% of each run, Pallas kernels for 0% -> 24%
where the time goes in v1:
time: 446 us; the launch traced here: 439 us
  waiting for transfers between devices  156 us (35%)
  Pallas kernels  107 us (24%)
  starting transfers between devices  70.4 us (16%)
  matrix products  56.6 us (13%)
  local copies, waits for them, and re-layouts  25.9 us (6%)
  other arithmetic  20.6 us (5%)
    ppermute x63, waiting for transfers between devices, swap(): return lax.ppermute(value, axis, [(i, i ^ distance) for i in range(size)])  156 us
    ppermute x63, starting transfers between devices, swap(): return lax.ppermute(value, axis, [(i, i ^ distance) for i in range(size)])  69.3 us
    pallas_call x4, Pallas kernels, attend_back(): pl.pallas_call(attend_back_kernel, grid_spec=spec, out_shape=[jax.ShapeDt...  60.4 us
    dot_general x24, matrix products, dot(): lax.dot_general(a, b, (((ca,), (cb,)), ((), ())), preferred_element_type=...  56.6 us
    pallas_call x4, Pallas kernels, attend(): pl.pallas_call(attend_kernel, grid_spec=spec, out_shape=[jax.ShapeDtypeSt...  46.9 us
  transfers between devices with their start and end apart: 65, of which 22 were waited for; matrix products, arithmetic and copies ran while one was open for 20% of the time, Pallas kernels for 24%

profile of v1, /device:TPU:0, one launch (start us, length us, event | category | flops | bytes accessed | tf_op | source)
XLA Modules:
  0.0 438.8 jit_solution(11254990531153244399)
XLA Ops:
  15.7 12.8 %attend.4 = (f32[3,200,640]{2,1,0:T(8,128)}, bf16[3,384,200]{2,1,0:T(8,128)(2,1)}, bf16[2,2400,128]{2,1,0:T(8,128)(2,1)}, bf16[2,2400,128]{2,1,0:T(8,128)(2,1)}, bf16[3,192,200]{2,1,0:T(8,128)(2,1)}) custom-call(s32[3]{0:T(128)} %pad_add_fusion.4.place, bf16[12,200,640]{2,1,0:T(8,128)(2,1)} %bitcast.102, bf16[3,800,640]{2,1,0:T(8,128)(2,1)} %row_ref.15, ...), custom_call_target="tpu_custom_call" | custom-call | flops 737280000 | bytes 8388608 | tf_op jit(solution)/shard_map/attend/pallas_call | solution.py:204
  40.7 39.0 %collective-permute-done.2.out_ref = bf16[192,640]{1,0:T(8,128)(2,1)} collective-permute-done((bf16[192,640]{1,0:T(8,128)(2,1)}, bf16[192,640]{1,0:T(8,128)(2,1)}, u32[]{:S(2)}, u32[]{:S(2)}) %collective-permute-start.2) | collective-permute-done | bytes 245792 | tf_op jit(solution)/shard_map/ppermute | solution.py:283
  80.6 12.6 %attend.5 = (f32[3,200,640]{2,1,0:T(8,128)}, bf16[3,384,200]{2,1,0:T(8,128)(2,1)}, bf16[2,2400,128]{2,1,0:T(8,128)(2,1)}, bf16[2,2400,128]{2,1,0:T(8,128)(2,1)}, bf16[3,192,200]{2,1,0:T(8,128)(2,1)}) custom-call(s32[3]{0:T(128)} %pad_add_fusion.3.place, bf16[12,200,640]{2,1,0:T(8,128)(2,1)} %bitcast.103, bf16[3,800,640]{2,1,0:T(8,128)(2,1)} %row_ref.15, ...), custom_call_target="tpu_custom_call" | custom-call | flops 737280000 | bytes 8388608 | tf_op jit(solution)/shard_map/attend/pallas_call | solution.py:204
  93.2 10.7 %attend.6 = (f32[3,200,640]{2,1,0:T(8,128)}, bf16[3,384,200]{2,1,0:T(8,128)(2,1)}, bf16[2,2400,128]{2,1,0:T(8,128)(2,1)}, bf16[2,2400,128]{2,1,0:T(8,128)(2,1)}, bf16[3,192,200]{2,1,0:T(8,128)(2,1)}) custom-call(s32[3]{0:T(128)} %pad_add_fusion.2.place, bf16[12,200,640]{2,1,0:T(8,128)(2,1)} %bitcast.104, bf16[3,800,640]{2,1,0:T(8,128)(2,1)} %row_ref.15, ...), custom_call_target="tpu_custom_call" | custom-call | flops 737280000 | bytes 8388608 | tf_op jit(solution)/shard_map/attend/pallas_call | solution.py:204
  107.5 10.8 %attend.7 = (f32[3,200,640]{2,1,0:T(8,128)}, bf16[3,384,200]{2,1,0:T(8,128)(2,1)}, bf16[2,2400,128]{2,1,0:T(8,128)(2,1)}, bf16[2,2400,128]{2,1,0:T(8,128)(2,1)}, bf16[3,192,200]{2,1,0:T(8,128)(2,1)}) custom-call(s32[3]{0:T(128)} %pad_add_fusion.place, bf16[12,200,640]{2,1,0:T(8,128)(2,1)} %bitcast.105, bf16[3,800,640]{2,1,0:T(8,128)(2,1)} %row_ref.15, ...), custom_call_target="tpu_custom_call" | custom-call | flops 737280000 | bytes 8388608 | tf_op jit(solution)/shard_map/attend/pallas_call | solution.py:204
  121.0 4.3 multiply_convert_fusion.3
  125.3 5.9 %multiply_convert_fusion.1 = (bf16[600,672]{0,1:T(8,128)(2,1)S(1)}, f32[600,672]{0,1:T(8,128)S(1)}, f32[600,672]{0,1:T(8,128)S(1)}) fusion(f32[672]{0:T(1024)S(1)} %slice_reduce_fusion.1, bf16[600,640]{1,0:T(8,128)(2,1)S(1)} %fusion.32, bf16[672,640]{1,0:T(8,128)(2,1)} %collective-permute-done.11), kind=kOutput, calls=%fused_computation.43 | convolution fusion | flops 542707200 | bytes 5662848 | tf_op jit(solution)/shard_map/dot_general | solution.py:22
  131.2 5.9 %multiply_convert_fusion.2 = (bf16[600,672]{0,1:T(8,128)(2,1)S(1)}, f32[600,672]{0,1:T(8,128)S(1)}, f32[600,672]{0,1:T(8,128)S(1)}) fusion(f32[672]{0:T(1024)S(1)} %slice_reduce_fusion.2, bf16[600,640]{1,0:T(8,128)(2,1)S(1)} %fusion.32, bf16[672,640]{1,0:T(8,128)(2,1)} %collective-permute-done.9), kind=kOutput, calls=%fused_computation.56 | convolution fusion | flops 542707200 | bytes 5662848 | tf_op jit(solution)/shard_map/dot_general | solution.py:22
  142.3 6.1 %multiply_convert_fusion = (bf16[600,672]{0,1:T(8,128)(2,1)S(1)}, f32[600,672]{0,1:T(8,128)S(1)}, f32[600,672]{0,1:T(8,128)S(1)}) fusion(f32[672]{0:T(1024)S(1)} %slice_reduce_fusion, bf16[600,640]{1,0:T(8,128)(2,1)S(1)} %fusion.32, bf16[672,640]{1,0:T(8,128)(2,1)} %collective-permute-done.13), kind=kOutput, calls=%fused_computation.30 | convolution fusion | flops 542707200 | bytes 5662848 | tf_op jit(solution)/shard_map/dot_general | solution.py:22
  180.2 14.0 %attend_back.4 = (bf16[768,640]{1,0:T(8,128)(2,1)}, f32[192,1]{1,0:T(8,128)}, f32[1,192]{1,0:T(1,128)}, f32[3,200,640]{2,1,0:T(8,128)}, f32[2,800,640]{2,1,0:T(8,128)}) custom-call(s32[3]{0:T(128)} %pad_add_fusion.place, bf16[12,200,640]{2,1,0:T(8,128)(2,1)} %bitcast.107, bf16[3,800,640]{2,1,0:T(8,128)(2,1)} %row_ref.15, ...), custom_call_target="tpu_custom_call", output_to_operand_aliasing={{4}: (11, {})} | custom-call | flops 1843200000 | bytes 8388608 | tf_op jit(solution)/shard_map/attend_back/pallas_call | solution.py:263
  194.2 14.0 %attend_back.5 = (bf16[768,640]{1,0:T(8,128)(2,1)}, f32[192,1]{1,0:T(8,128)}, f32[1,192]{1,0:T(1,128)}, f32[3,200,640]{2,1,0:T(8,128)}, f32[2,800,640]{2,1,0:T(8,128)}) custom-call(s32[3]{0:T(128)} %pad_add_fusion.2.place, bf16[12,200,640]{2,1,0:T(8,128)(2,1)} %bitcast.108, bf16[3,800,640]{2,1,0:T(8,128)(2,1)} %row_ref.15, ...), custom_call_target="tpu_custom_call", output_to_operand_aliasing={{4}: (11, {})} | custom-call | flops 1843200000 | bytes 8388608 | tf_op jit(solution)/shard_map/attend_back/pallas_call | solution.py:263
  208.2 16.2 %attend_back.6 = (bf16[768,640]{1,0:T(8,128)(2,1)}, f32[192,1]{1,0:T(8,128)}, f32[1,192]{1,0:T(1,128)}, f32[3,200,640]{2,1,0:T(8,128)}, f32[2,800,640]{2,1,0:T(8,128)}) custom-call(s32[3]{0:T(128)} %pad_add_fusion.3.place, bf16[12,200,640]{2,1,0:T(8,128)(2,1)} %bitcast.109, bf16[3,800,640]{2,1,0:T(8,128)(2,1)} %row_ref.15, ...), custom_call_target="tpu_custom_call", output_to_operand_aliasing={{4}: (11, {})} | custom-call | flops 1843200000 | bytes 8388608 | tf_op jit(solution)/shard_map/attend_back/pallas_call | solution.py:263
  224.5 16.2 %attend_back.7 = (bf16[768,640]{1,0:T(8,128)(2,1)}, f32[192,1]{1,0:T(8,128)}, f32[1,192]{1,0:T(1,128)}, f32[3,200,640]{2,1,0:T(8,128)}, f32[2,800,640]{2,1,0:T(8,128)}) custom-call(s32[3]{0:T(128)} %pad_add_fusion.4.place, bf16[12,200,640]{2,1,0:T(8,128)(2,1)} %bitcast.110, bf16[3,800,640]{2,1,0:T(8,128)(2,1)} %row_ref.15, ...), custom_call_target="tpu_custom_call", output_to_operand_aliasing={{4}: (11, {})} | custom-call | flops 1843200000 | bytes 8388608 | tf_op jit(solution)/shard_map/attend_back/pallas_call | solution.py:263
  241.9 6.4 %collective-permute-start.32 = (f32[1,384]{1,0:T(1,128)S(1)}, f32[1,384]{1,0:T(1,128)S(1)}, u32[]{:S(2)}, u32[]{:S(2)}) collective-permute-start(f32[1,384]{1,0:T(1,128)S(1)} %broadcast_in_dim.106), channel_id=1, source_target_pairs={{0,1},{1,0},{2,3},{3,2},{4,5},{5,4},{6,7},{7,6},{8,9},{9,8},{10,11... | collective-permute-start | bytes 4616 | tf_op jit(solution)/shard_map/ppermute | solution.py:283
  296.0 12.6 %collective-permute-done.21 = bf16[600,640]{1,0:T(8,128)(2,1)S(1)} collective-permute-done((bf16[600,640]{1,0:T(8,128)(2,1)S(1)}, bf16[600,640]{1,0:T(8,128)(2,1)S(1)}, u32[]{:S(2)}, u32[]{:S(2)}) %collective-permute-start.21) | collective-permute-done | bytes 768032 | tf_op jit(solution)/shard_map/ppermute | solution.py:283
  310.4 16.6 %collective-permute-done.59 = bf16[672,640]{1,0:T(8,128)(2,1)S(1)} collective-permute-done((bf16[672,640]{1,0:T(8,128)(2,1)S(1)}, bf16[672,640]{1,0:T(8,128)(2,1)S(1)}, u32[]{:S(2)}, u32[]{:S(2)}) %collective-permute-start.59) | collective-permute-done | bytes 860192 | tf_op jit(solution)/shard_map/ppermute | solution.py:283
  328.9 16.6 %collective-permute-done.45 = bf16[672,640]{1,0:T(8,128)(2,1)S(1)} collective-permute-done((bf16[672,640]{1,0:T(8,128)(2,1)S(1)}, bf16[672,640]{1,0:T(8,128)(2,1)S(1)}, u32[]{:S(2)}, u32[]{:S(2)}) %collective-permute-start.45) | collective-permute-done | bytes 860192 | tf_op jit(solution)/shard_map/ppermute | solution.py:283
  347.3 18.6 %collective-permute-done.25 = bf16[768,640]{1,0:T(8,128)(2,1)S(1)} collective-permute-done((bf16[768,640]{1,0:T(8,128)(2,1)S(1)}, bf16[768,640]{1,0:T(8,128)(2,1)S(1)}, u32[]{:S(2)}, u32[]{:S(2)}) %collective-permute-start.25) | collective-permute-done | bytes 983072 | tf_op jit(solution)/shard_map/ppermute | solution.py:283
  370.3 8.1 %collective-permute-done.61 = bf16[168,640]{1,0:T(8,128)(2,1)S(1)} collective-permute-done((bf16[168,640]{1,0:T(8,128)(2,1)S(1)}, bf16[168,640]{1,0:T(8,128)(2,1)S(1)}, u32[]{:S(2)}, u32[]{:S(2)}) %collective-permute-start.61) | collective-permute-done | bytes 215072 | tf_op jit(solution)/shard_map/ppermute | solution.py:283
  385.4 8.9 %collective-permute-done.62 = bf16[168,640]{1,0:T(8,128)(2,1)S(1)} collective-permute-done((bf16[168,640]{1,0:T(8,128)(2,1)S(1)}, bf16[168,640]{1,0:T(8,128)(2,1)S(1)}, u32[]{:S(2)}, u32[]{:S(2)}) %collective-permute-start.62) | collective-permute-done | bytes 215072 | tf_op jit(solution)/shard_map/ppermute | solution.py:283
  399.0 5.2 %collective-permute-done.63 = bf16[168,640]{1,0:T(8,128)(2,1)S(1)} collective-permute-done((bf16[168,640]{1,0:T(8,128)(2,1)S(1)}, bf16[168,640]{1,0:T(8,128)(2,1)S(1)}, u32[]{:S(2)}, u32[]{:S(2)}) %collective-permute-start.63) | collective-permute-done | bytes 215072 | tf_op jit(solution)/shard_map/ppermute | solution.py:283
  410.9 3.8 collective-permute-start.30
  422.6 7.4 %collective-permute-done.50 = bf16[336,640]{1,0:T(8,128)(2,1)S(1)} collective-permute-done((bf16[336,640]{1,0:T(8,128)(2,1)S(1)}, bf16[336,640]{1,0:T(8,128)(2,1)S(1)}, u32[]{:S(2)}, u32[]{:S(2)}) %collective-permute-start.50) | collective-permute-done | bytes 430112 | tf_op jit(solution)/shard_map/ppermute | solution.py:283
  432.1 4.6 %collective-permute-done.31 = bf16[384,640]{1,0:T(8,128)(2,1)S(1)} collective-permute-done((bf16[384,640]{1,0:T(8,128)(2,1)S(1)}, bf16[384,640]{1,0:T(8,128)(2,1)S(1)}, u32[]{:S(2)}, u32[]{:S(2)}) %collective-permute-start.31) | collective-permute-done | bytes 491552 | tf_op jit(solution)/shard_map/ppermute | solution.py:283
  (376 shorter events, 159.1 us)
Async XLA Ops:
  1.5 33.1 %collective-permute-start.8 = (f32[1,1056]{1,0:T(1,128)S(1)}, f32[1,1056]{1,0:T(1,128)S(1)}, u32[]{:S(2)}, u32[]{:S(2)}) collective-permute-start(f32[1,1056]{1,0:T(1,128)S(1)} %broadcast_in_dim.95), channel_id=1, source_target_pairs={{0,1},{1,0},{2,3},{3,2},{4,5},{5,4},{6,7},{7,6},{8,9},{9,8},{10,11... | collective-permute-start | bytes 12680 | tf_op jit(solution)/shard_map/ppermute | solution.py:283
  1.9 30.4 %collective-permute-start.4 = (f32[1,1056]{1,0:T(1,128)S(1)}, f32[1,1056]{1,0:T(1,128)S(1)}, u32[]{:S(2)}, u32[]{:S(2)}) collective-permute-start(f32[1,1056]{1,0:T(1,128)S(1)} %broadcast_in_dim.95), channel_id=1, source_target_pairs={{0,2},{1,3},{2,0},{3,1},{4,6},{5,7},{6,4},{7,5},{8,10},{9,11},{10,... | collective-permute-start | bytes 12680 | tf_op jit(solution)/shard_map/ppermute | solution.py:283
  5.7 73.9 %collective-permute-start.6 = (bf16[576,640]{1,0:T(8,128)(2,1)S(1)}, bf16[576,640]{1,0:T(8,128)(2,1)S(1)}, u32[]{:S(2)}, u32[]{:S(2)}) collective-permute-start(bf16[576,640]{1,0:T(8,128)(2,1)S(1)} %pad_maximum_fusion.qkv_ref), channel_id=1, source_target_pairs={{0,1},{1,0},{2,3},{3,2},{4,5},{5,4},{6,7},{7,6},{8,9},{9,8},{10,11... | collective-permute-start | bytes 2211848 | tf_op jit(solution)/shard_map/ppermute | solution.py:283
  6.0 30.7 %collective-permute-start = (bf16[576,640]{1,0:T(8,128)(2,1)S(1)}, bf16[576,640]{1,0:T(8,128)(2,1)S(1)}, u32[]{:S(2)}, u32[]{:S(2)}) collective-permute-start(bf16[576,640]{1,0:T(8,128)(2,1)S(1)} %pad_maximum_fusion.qkv_ref), channel_id=1, source_target_pairs={{0,2},{1,3},{2,0},{3,1},{4,6},{5,7},{6,4},{7,5},{8,10},{9,11},{10,... | collective-permute-start | bytes 2211848 | tf_op jit(solution)/shard_map/ppermute | solution.py:283
  8.0 29.4 %collective-permute-start.7 = (bf16[192,640]{1,0:T(8,128)(2,1)}, bf16[192,640]{1,0:T(8,128)(2,1)S(1)}, u32[]{:S(2)}, u32[]{:S(2)}) collective-permute-start(bf16[192,640]{1,0:T(8,128)(2,1)} %broadcast_select_fusion.9.out_ref), channel_id=1, source_target_pairs={{0,1},{1,0},{2,3},{3,2},{4,5},{5,4},{6,7},{7,6},{8,9},{9,8},{10,11... | collective-permute-start | bytes 737288 | tf_op jit(solution)/shard_map/ppermute | solution.py:283
  34.6 72.3 %collective-permute-start.11 = (bf16[672,640]{1,0:T(8,128)(2,1)}, bf16[672,640]{1,0:T(8,128)(2,1)}, u32[]{:S(2)}, u32[]{:S(2)}) collective-permute-start(bf16[672,640]{1,0:T(8,128)(2,1)} %slice.176), channel_id=1, source_target_pairs={{0,2},{1,3},{2,0},{3,1},{4,6},{5,7},{6,4},{7,5},{8,10},{9,11},{10,... | collective-permute-start | bytes 2580488 | tf_op jit(solution)/shard_map/ppermute | solution.py:283
  34.8 72.2 %collective-permute-start.12 = (bf16[672,640]{1,0:T(8,128)(2,1)}, bf16[672,640]{1,0:T(8,128)(2,1)}, u32[]{:S(2)}, u32[]{:S(2)}) collective-permute-start(bf16[672,640]{1,0:T(8,128)(2,1)} %slice_select_fusion), channel_id=1, source_target_pairs={{0,2},{1,3},{2,0},{3,1},{4,6},{5,7},{6,4},{7,5},{8,10},{9,11},{10,... | collective-permute-start | bytes 2580488 | tf_op jit(solution)/shard_map/ppermute | solution.py:283
  36.7 70.8 %collective-permute-start.1 = (bf16[576,640]{1,0:T(8,128)(2,1)S(1)}, bf16[576,640]{1,0:T(8,128)(2,1)}, u32[]{:S(2)}, u32[]{:S(2)}) collective-permute-start(bf16[576,640]{1,0:T(8,128)(2,1)S(1)} %collective-permute-done.qkv_ref), channel_id=1, source_target_pairs={{0,1},{1,0},{2,3},{3,2},{4,5},{5,4},{6,7},{7,6},{8,9},{9,8},{10,11... | collective-permute-start | bytes 2211848 | tf_op jit(solution)/shard_map/ppermute | solution.py:283
  37.4 42.2 %collective-permute-start.2 = (bf16[192,640]{1,0:T(8,128)(2,1)}, bf16[192,640]{1,0:T(8,128)(2,1)}, u32[]{:S(2)}, u32[]{:S(2)}) collective-permute-start(bf16[192,640]{1,0:T(8,128)(2,1)} %broadcast_select_fusion.9.out_ref), channel_id=1, source_target_pairs={{0,2},{1,3},{2,0},{3,1},{4,6},{5,7},{6,4},{7,5},{8,10},{9,11},{10,... | collective-permute-start | bytes 737288 | tf_op jit(solution)/shard_map/ppermute | solution.py:283
  79.7 24.3 %collective-permute-start.3 = (bf16[192,640]{1,0:T(8,128)(2,1)}, bf16[192,640]{1,0:T(8,128)(2,1)}, u32[]{:S(2)}, u32[]{:S(2)}) collective-permute-start(bf16[192,640]{1,0:T(8,128)(2,1)} %collective-permute-done.2.out_ref), channel_id=1, source_target_pairs={{0,1},{1,0},{2,3},{3,2},{4,5},{5,4},{6,7},{7,6},{8,9},{9,8},{10,11... | collective-permute-start | bytes 737288 | tf_op jit(solution)/shard_map/ppermute | solution.py:283
  79.7 51.5 %collective-permute-start.9 = (bf16[672,640]{1,0:T(8,128)(2,1)}, bf16[672,640]{1,0:T(8,128)(2,1)}, u32[]{:S(2)}, u32[]{:S(2)}) collective-permute-start(bf16[672,640]{1,0:T(8,128)(2,1)} %slice.176), channel_id=1, source_target_pairs={{0,1},{1,0},{2,3},{3,2},{4,5},{5,4},{6,7},{7,6},{8,9},{9,8},{10,11... | collective-permute-start | bytes 2580488 | tf_op jit(solution)/shard_map/ppermute | solution.py:283
  104.0 36.2 %collective-permute-start.10 = (bf16[672,640]{1,0:T(8,128)(2,1)S(1)}, bf16[672,640]{1,0:T(8,128)(2,1)}, u32[]{:S(2)}, u32[]{:S(2)}) collective-permute-start(bf16[672,640]{1,0:T(8,128)(2,1)S(1)} %copy-done.11), channel_id=1, source_target_pairs={{0,1},{1,0},{2,3},{3,2},{4,5},{5,4},{6,7},{7,6},{8,9},{9,8},{10,11... | collective-permute-start | bytes 2580488 | tf_op jit(solution)/shard_map/ppermute | solution.py:283
  106.9 35.4 %collective-permute-start.13 = (bf16[672,640]{1,0:T(8,128)(2,1)}, bf16[672,640]{1,0:T(8,128)(2,1)}, u32[]{:S(2)}, u32[]{:S(2)}) collective-permute-start(bf16[672,640]{1,0:T(8,128)(2,1)} %collective-permute-done.11), channel_id=1, source_target_pairs={{0,1},{1,0},{2,3},{3,2},{4,5},{5,4},{6,7},{7,6},{8,9},{9,8},{10,11... | collective-permute-start | bytes 2580488 | tf_op jit(solution)/shard_map/ppermute | solution.py:283
  107.0 41.4 %collective-permute-start.14 = (bf16[672,640]{1,0:T(8,128)(2,1)}, bf16[672,640]{1,0:T(8,128)(2,1)}, u32[]{:S(2)}, u32[]{:S(2)}) collective-permute-start(bf16[672,640]{1,0:T(8,128)(2,1)} %collective-permute-done.12), channel_id=1, source_target_pairs={{0,1},{1,0},{2,3},{3,2},{4,5},{5,4},{6,7},{7,6},{8,9},{9,8},{10,11... | collective-permute-start | bytes 2580488 | tf_op jit(solution)/shard_map/ppermute | solution.py:283
  159.4 91.8 %collective-permute-start.52 = (f32[672]{0:T(1024)S(1)}, f32[672]{0:T(1024)S(1)}, u32[]{:S(2)}, u32[]{:S(2)}) collective-permute-start(f32[672]{0:T(1024)S(1)} %get-tuple-element.166), channel_id=1, source_target_pairs={{0,1},{1,0},{2,3},{3,2},{4,5},{5,4},{6,7},{7,6},{8,9},{9,8},{10,11... | collective-permute-start | bytes 8072 | tf_op jit(solution)/shard_map/ppermute | solution.py:283
  163.2 91.9 %collective-permute-start.51 = (f32[672]{0:T(1024)S(1)}, f32[672]{0:T(1024)S(1)}, u32[]{:S(2)}, u32[]{:S(2)}) collective-permute-start(f32[672]{0:T(1024)S(1)} %get-tuple-element.162), channel_id=1, source_target_pairs={{0,1},{1,0},{2,3},{3,2},{4,5},{5,4},{6,7},{7,6},{8,9},{9,8},{10,11... | collective-permute-start | bytes 8072 | tf_op jit(solution)/shard_map/ppermute | solution.py:283
  176.7 79.9 %collective-permute-start.38 = (f32[6,640]{1,0:T(8,128)S(1)}, f32[6,640]{1,0:T(8,128)S(1)}, u32[]{:S(2)}, u32[]{:S(2)}) collective-permute-start(f32[6,640]{1,0:T(8,128)S(1)} %stack.66), channel_id=1, source_target_pairs={{0,1},{1,0},{2,3},{3,2},{4,5},{5,4},{6,7},{7,6},{8,9},{9,8},{10,11... | collective-permute-start | bytes 46088 | tf_op jit(solution)/shard_map/ppermute | solution.py:283
  292.4 34.7 %collective-permute-start.59 = (bf16[672,640]{1,0:T(8,128)(2,1)S(1)}, bf16[672,640]{1,0:T(8,128)(2,1)S(1)}, u32[]{:S(2)}, u32[]{:S(2)}) collective-permute-start(bf16[672,640]{1,0:T(8,128)(2,1)S(1)} %add_convert_fusion.4), channel_id=1, source_target_pairs={{0,2},{1,3},{2,0},{3,1},{4,6},{5,7},{6,4},{7,5},{8,10},{9,11},{10,... | collective-permute-start | bytes 2580488 | tf_op jit(solution)/shard_map/ppermute | solution.py:283
  293.7 53.6 %collective-permute-start.23 = (bf16[768,640]{1,0:T(8,128)(2,1)S(1)}, bf16[768,640]{1,0:T(8,128)(2,1)S(1)}, u32[]{:S(2)}, u32[]{:S(2)}) collective-permute-start(bf16[768,640]{1,0:T(8,128)(2,1)S(1)} %copy-done.33), channel_id=1, source_target_pairs={{0,1},{1,0},{2,3},{3,2},{4,5},{5,4},{6,7},{7,6},{8,9},{9,8},{10,11... | collective-permute-start | bytes 2949128 | tf_op jit(solution)/shard_map/ppermute | solution.py:283
  294.3 51.2 %collective-permute-start.45 = (bf16[672,640]{1,0:T(8,128)(2,1)S(1)}, bf16[672,640]{1,0:T(8,128)(2,1)S(1)}, u32[]{:S(2)}, u32[]{:S(2)}) collective-permute-start(bf16[672,640]{1,0:T(8,128)(2,1)S(1)} %add_convert_fusion.7), channel_id=1, source_target_pairs={{0,2},{1,3},{2,0},{3,1},{4,6},{5,7},{6,4},{7,5},{8,10},{9,11},{10,... | collective-permute-start | bytes 2580488 | tf_op jit(solution)/shard_map/ppermute | solution.py:283
  308.6 57.3 %collective-permute-start.25 = (bf16[768,640]{1,0:T(8,128)(2,1)S(1)}, bf16[768,640]{1,0:T(8,128)(2,1)S(1)}, u32[]{:S(2)}, u32[]{:S(2)}) collective-permute-start(bf16[768,640]{1,0:T(8,128)(2,1)S(1)} %add_convert_fusion.1), channel_id=1, source_target_pairs={{0,2},{1,3},{2,0},{3,1},{4,6},{5,7},{6,4},{7,5},{8,10},{9,11},{10,... | collective-permute-start | bytes 2949128 | tf_op jit(solution)/shard_map/ppermute | solution.py:283
  310.2 59.9 %collective-permute-start.22 = (bf16[600,640]{1,0:T(8,128)(2,1)S(1)}, bf16[600,640]{1,0:T(8,128)(2,1)S(1)}, u32[]{:S(2)}, u32[]{:S(2)}) collective-permute-start(bf16[600,640]{1,0:T(8,128)(2,1)S(1)} %collective-permute-done.21), channel_id=1, source_target_pairs={{0,1},{1,0},{2,3},{3,2},{4,5},{5,4},{6,7},{7,6},{8,9},{9,8},{10,11... | collective-permute-start | bytes 2304008 | tf_op jit(solution)/shard_map/ppermute | solution.py:283
  327.4 40.2 %collective-permute-start.60 = (bf16[336,640]{1,0:T(8,128)(2,1)S(1)}, bf16[336,640]{1,0:T(8,128)(2,1)S(1)}, u32[]{:S(2)}, u32[]{:S(2)}) collective-permute-start(bf16[336,640]{1,0:T(8,128)(2,1)S(1)} %broadcast_select_fusion.5), channel_id=1, source_target_pairs={{0,4},{4,0},{8,12},{12,8},{16,20},{20,16},{24,28},{28,24},{1,5},{5... | collective-permute-start | bytes 1290248 | tf_op jit(solution)/shard_map/ppermute | solution.py:283
  345.8 23.6 %collective-permute-start.46 = (bf16[336,640]{1,0:T(8,128)(2,1)S(1)}, bf16[336,640]{1,0:T(8,128)(2,1)S(1)}, u32[]{:S(2)}, u32[]{:S(2)}) collective-permute-start(bf16[336,640]{1,0:T(8,128)(2,1)S(1)} %broadcast_select_fusion.8), channel_id=1, source_target_pairs={{0,4},{4,0},{8,12},{12,8},{16,20},{20,16},{24,28},{28,24},{1,5},{5... | collective-permute-start | bytes 1290248 | tf_op jit(solution)/shard_map/ppermute | solution.py:283
  (89 other events, 908.3 us)
